TPU v7x, 256 devices: a whole 4x4x8 slice. The times are simulated.
256 devices in a mesh: dp: 8 (over y, core), expert: 32 (over z, x).
Axes of the slice: x: 4, y: 4, z: 8, core: 2. Of those that a mesh axis runs over, the one named last changes fastest.
Arguments:
- tokens: bfloat16 [65536, 4096], P(('dp', 'expert')), may hold values from -6 to 6
- routes: int32 [65536, 2], P(('dp', 'expert')), may hold values from 0 to 31, all different within a row; in each aligned block of 256 rows (0 to 255, 256 to 511, ...) at most 32 rows name the same one
- route_weights: float32 [65536, 2], P(('dp', 'expert')), may hold values from 0.1 to 0.9
- placement: int32 [32], replicated, may hold values from 0 to 31, each once
- expert_weights: bfloat16 [32, 4096, 1024], P('expert', None, 'dp'), may hold values from -0.09375 to 0.09375
- grads: bfloat16 [32, 4096, 1024], P('expert', None, 'dp'), may hold values from -0.059814453 to 0.059814453
- first_moment: bfloat16 [32, 4096, 1024], P('expert', None, 'dp'), may hold values from -0.017944336 to 0.017944336
- second_moment: bfloat16 [32, 4096, 1024], P('expert', None, 'dp'), may hold values from 9.953976e-06 to 0.0009994507
Outputs:
- new_weights: bfloat16 [32, 4096, 1024], P('expert', None, 'dp')
- new_first: bfloat16 [32, 4096, 1024], P('expert', None, 'dp')
- new_second: bfloat16 [32, 4096, 1024], P('expert', None, 'dp')
- mixed: bfloat16 [65536, 1024], P(('dp', 'expert'))
Inputs may be any that keep to these rules, and one draw needn't show every extreme that they name: `routes`: each token names two different experts; within the rows of one device no expert is named more than 32 times, a bound that some block reaches. `placement`: each expert appears exactly once.
All inputs are finite; a program needn't handle non-finite values.
Results may differ from a plain program's by a relative error of at most 0.0057.
Values may be sent and summed in bfloat16 or wider, within the bound.
A program may use at most 192 MiB of HBM per device.

v0:
```python
import jax
import jax.numpy as jnp
from jax import lax
from jax.sharding import PartitionSpec as P

beta_one = 0.9
beta_two = 0.999
learn_rate = 0.008
adam_eps = 1e-08


def adam_step(weight, gradient, first, second):
    grad_wide = gradient.astype(jnp.float32)
    first_wide = beta_one * first.astype(jnp.float32) + (1.0 - beta_one) * grad_wide
    second_wide = beta_two * second.astype(jnp.float32) + (1.0 - beta_two) * grad_wide * grad_wide
    updated = weight.astype(jnp.float32) - learn_rate * first_wide / (
        jnp.sqrt(second_wide) + adam_eps
    )
    return (
        updated.astype(jnp.bfloat16),
        first_wide.astype(jnp.bfloat16),
        second_wide.astype(jnp.bfloat16),
    )


def to_pieces(slab, count):
    return slab.reshape(count, slab.shape[0] // count, slab.shape[1])


def from_pieces(pieces):
    return pieces.reshape(pieces.shape[0] * pieces.shape[1], pieces.shape[2])


def shards(
    tokens, routes, route_weights, placement, expert_weights, grads, first_moment, second_moment
):
    experts = lax.axis_size("expert")
    width = tokens.shape[1]
    spread = (
        lax.all_to_all(
            to_pieces(expert_weights[0], experts), "expert", split_axis=0, concat_axis=0, tiled=True
        ),
        lax.all_to_all(
            to_pieces(grads[0], experts), "expert", split_axis=0, concat_axis=0, tiled=True
        ),
        lax.all_to_all(
            to_pieces(first_moment[0], experts), "expert", split_axis=0, concat_axis=0, tiled=True
        ),
        lax.all_to_all(
            to_pieces(second_moment[0], experts), "expert", split_axis=0, concat_axis=0, tiled=True
        ),
    )
    chosen = tuple((jnp.take(member, placement, axis=0) for member in spread))
    collected = (
        lax.all_to_all(chosen[0], "expert", split_axis=0, concat_axis=0, tiled=True),
        lax.all_to_all(chosen[1], "expert", split_axis=0, concat_axis=0, tiled=True),
        lax.all_to_all(chosen[2], "expert", split_axis=0, concat_axis=0, tiled=True),
        lax.all_to_all(chosen[3], "expert", split_axis=0, concat_axis=0, tiled=True),
    )
    new_slab, first_slab, second_slab = adam_step(
        from_pieces(collected[0]),
        from_pieces(collected[1]),
        from_pieces(collected[2]),
        from_pieces(collected[3]),
    )
    tok_count = tokens.shape[0]
    capacity = 4 * tok_count // experts
    expert_ids = jnp.arange(experts, dtype=jnp.int32)
    entries = routes.reshape(2 * tok_count)
    onehot = (entries[:, None] == expert_ids[None, :]).astype(jnp.int32)
    before = jnp.cumsum(onehot, axis=0) - onehot
    position = jnp.sum(before * onehot, axis=1)
    hosting = jnp.sum(
        jnp.where(placement[None, :] == expert_ids[:, None], expert_ids[None, :], 0), axis=1
    )
    target_dev = jnp.sum(onehot * hosting[None, :], axis=1)
    target_slot = target_dev * capacity + position
    select = (
        target_slot[:, None] == jnp.arange(experts * capacity, dtype=jnp.int32)[None, :]
    ).astype(jnp.bfloat16)
    select_pairs = select.reshape(tok_count, 2, experts * capacity)
    select_tokens = jnp.sum(select_pairs, axis=1)
    outgoing = jnp.einsum(
        "ts,td->sd", select_tokens, tokens, preferred_element_type=jnp.float32
    ).astype(jnp.bfloat16)
    received = lax.all_to_all(
        outgoing.reshape(experts, capacity, width),
        "expert",
        split_axis=0,
        concat_axis=0,
        tiled=True,
    )
    slot_rows = received.reshape(experts * capacity, width)
    acts = jax.nn.silu(
        jnp.dot(
            slot_rows,
            lax.all_gather(new_slab, "dp", axis=1, tiled=True),
            preferred_element_type=jnp.float32,
        )
    ).astype(jnp.bfloat16)
    hidden = acts.shape[1]
    returned = lax.all_to_all(
        acts.reshape(experts, capacity, hidden), "expert", split_axis=0, concat_axis=0, tiled=True
    )
    back_rows = returned.reshape(experts * capacity, hidden)
    picked = jnp.einsum("tks,sh->tkh", select_pairs, back_rows, preferred_element_type=jnp.float32)
    mixed = jnp.sum(route_weights[:, :, None] * picked, axis=1).astype(jnp.bfloat16)
    return (new_slab[None], first_slab[None], second_slab[None], mixed)


def solution(mesh):
    return jax.shard_map(
        shards,
        mesh=mesh,
        in_specs=(
            P(("dp", "expert"), None),
            P(("dp", "expert"), None),
            P(("dp", "expert"), None),
            P(),
            P("expert", None, "dp"),
            P("expert", None, "dp"),
            P("expert", None, "dp"),
            P("expert", None, "dp"),
        ),
        out_specs=(
            P("expert", None, "dp"),
            P("expert", None, "dp"),
            P("expert", None, "dp"),
            P(("dp", "expert"), None),
        ),
        check_vma=False,
    )
```

profile of v0, /device:TPU:1, one launch (start us, length us, event | category | flops | bytes accessed | tf_op | source)
XLA Modules:
  0.0 537.2 jit_solution(310885808594735539)
XLA Ops:
  7.2 38.5 %all_to_all.50 = bf16[32,128,128]{2,1,0:T(8,128)(2,1)} all-to-all(bf16[32,128,128]{2,1,0:T(8,128)(2,1)} %bitcast.99), channel_id=1, replica_groups=mesh['dp'=8,'expert'=32] {'expert'}, dimensions={0} | all-to-all | bytes 2097152 | tf_op jit(solution)/shard_map/all_to_all | solution.py:49
  45.7 31.5 %all_to_all.51 = bf16[32,128,128]{2,1,0:T(8,128)(2,1)} all-to-all(bf16[32,128,128]{2,1,0:T(8,128)(2,1)S(1)} %bitcast.100), channel_id=1, replica_groups=mesh['dp'=8,'expert'=32] {'expert'}, dimensions={0} | all-to-all | bytes 2097152 | tf_op jit(solution)/shard_map/all_to_all | solution.py:46
  77.2 31.2 %all_to_all.52 = bf16[32,128,128]{2,1,0:T(8,128)(2,1)} all-to-all(bf16[32,128,128]{2,1,0:T(8,128)(2,1)S(1)} %bitcast.101), channel_id=1, replica_groups=mesh['dp'=8,'expert'=32] {'expert'}, dimensions={0} | all-to-all | bytes 2097152 | tf_op jit(solution)/shard_map/all_to_all | solution.py:43
  108.4 7.5 %all-to-all-start = ((bf16[32,128,128]{2,1,0:T(8,128)(2,1)}), bf16[32,128,128]{2,1,0:T(8,128)(2,1)}, u32[]{:S(2)}, u32[]{:S(2)}) async-start(bf16[32,128,128]{2,1,0:T(8,128)(2,1)} %bitcast), calls=%async_computation | async-start | bytes 2097152 | tf_op jit(solution)/shard_map/all_to_all | solution.py:40
  116.0 2.0 gather_fusion.3
  118.0 2.9 gather_fusion.1
  120.9 2.9 gather_fusion.2
  123.8 16.6 %all-to-all-done = bf16[32,128,128]{2,1,0:T(8,128)(2,1)} async-done(((bf16[32,128,128]{2,1,0:T(8,128)(2,1)}), bf16[32,128,128]{2,1,0:T(8,128)(2,1)}, u32[]{:S(2)}, u32[]{:S(2)}) %all-to-all-start) | async-done | bytes 1048608 | tf_op jit(solution)/shard_map/all_to_all | solution.py:40
  140.4 2.9 gather_fusion
  143.3 3.3 broadcast_select_fusion
  146.5 31.0 %all_to_all.53 = bf16[32,128,128]{2,1,0:T(8,128)(2,1)S(1)} all-to-all(bf16[32,128,128]{2,1,0:T(8,128)(2,1)S(1)} %get-tuple-element.12), channel_id=1, replica_groups=mesh['dp'=8,'expert'=32] {'expert'}, dimensions={0} | all-to-all | bytes 2097152 | tf_op jit(solution)/shard_map/all_to_all | solution.py:56
  177.5 30.3 %all_to_all.54 = bf16[32,128,128]{2,1,0:T(8,128)(2,1)} all-to-all(bf16[32,128,128]{2,1,0:T(8,128)(2,1)S(1)} %get-tuple-element.10), channel_id=1, replica_groups=mesh['dp'=8,'expert'=32] {'expert'}, dimensions={0} | all-to-all | bytes 2097152 | tf_op jit(solution)/shard_map/all_to_all | solution.py:58
  207.8 30.1 %all_to_all.55 = bf16[32,128,128]{2,1,0:T(8,128)(2,1)} all-to-all(bf16[32,128,128]{2,1,0:T(8,128)(2,1)S(1)} %get-tuple-element.11), channel_id=1, replica_groups=mesh['dp'=8,'expert'=32] {'expert'}, dimensions={0} | all-to-all | bytes 2097152 | tf_op jit(solution)/shard_map/all_to_all | solution.py:57
  238.0 6.7 %all-to-all-start.1 = ((bf16[32,128,128]{2,1,0:T(8,128)(2,1)}), bf16[32,128,128]{2,1,0:T(8,128)(2,1)}, u32[]{:S(2)}, u32[]{:S(2)}) async-start(bf16[32,128,128]{2,1,0:T(8,128)(2,1)} %get-tuple-element.13), calls=%async_computation.1 | async-start | bytes 2097152 | tf_op jit(solution)/shard_map/all_to_all | solution.py:55
  245.2 1.2 reduce-window.6
  247.1 0.3 fusion.17
  247.3 5.6 %convolution_convert_fusion = bf16[1024,4096]{1,0:T(8,128)(2,1)} fusion(bf16[256,1024]{1,0:T(8,128)(2,1)S(1)} %fusion.17, bf16[256,4096]{1,0:T(8,128)(2,1)S(1)} %copy-done), kind=kOutput, calls=%fused_computation.4 | convolution fusion | flops 2151677952 | bytes 11010048 | tf_op jit(solution)/shard_map/ts,td->sd/dot_general | solution.py:83
  253.0 14.2 %all-to-all-done.1 = bf16[32,128,128]{2,1,0:T(8,128)(2,1)} async-done(((bf16[32,128,128]{2,1,0:T(8,128)(2,1)}), bf16[32,128,128]{2,1,0:T(8,128)(2,1)}, u32[]{:S(2)}, u32[]{:S(2)}) %all-to-all-start.1) | async-done | bytes 1048608 | tf_op jit(solution)/shard_map/all_to_all | solution.py:55
  267.2 7.7 %all-to-all-start.8 = ((bf16[32,32,4096]{2,1,0:T(8,128)(2,1)}), bf16[32,32,4096]{2,1,0:T(8,128)(2,1)}, u32[]{:S(2)}, u32[]{:S(2)}) async-start(bf16[32,32,4096]{2,1,0:T(8,128)(2,1)} %bitcast.93), calls=%async_computation.8 | async-start | bytes 16777216 | tf_op jit(solution)/shard_map/all_to_all | solution.py:86
  275.1 1.6 convert_multiply_fusion
  276.7 0.2 convert_multiply_fusion.1
  277.0 1.1 copy-done.1
  278.1 1.3 copy-done.3
  279.4 3.8 fusion.10
  283.2 171.4 %all-to-all-done.8 = bf16[32,32,4096]{2,1,0:T(8,128)(2,1)} async-done(((bf16[32,32,4096]{2,1,0:T(8,128)(2,1)}), bf16[32,32,4096]{2,1,0:T(8,128)(2,1)}, u32[]{:S(2)}, u32[]{:S(2)}) %all-to-all-start.8) | async-done | bytes 8388640 | tf_op jit(solution)/shard_map/all_to_all | solution.py:86
  454.6 15.3 %multiply_convert_fusion = bf16[1024,1024]{1,0:T(8,128)(2,1)} fusion(bf16[1024,4096]{1,0:T(8,128)(2,1)} %bitcast.11, bf16[4096,1024]{1,0:T(8,128)(2,1)} %all-gather.2.cloned.1.call-done), kind=kOutput, calls=%fused_computation.5 | convolution fusion | flops 8595177472 | bytes 18874368 | tf_op jit(solution)/shard_map/dot_general | solution.py:95
  469.9 10.6 %all-to-all-start.9 = ((bf16[32,32,1024]{2,1,0:T(8,128)(2,1)}), bf16[32,32,1024]{2,1,0:T(8,128)(2,1)}, u32[]{:S(2)}, u32[]{:S(2)}) async-start(bf16[32,32,1024]{2,1,0:T(8,128)(2,1)} %bitcast.98), calls=%async_computation.9 | async-start | bytes 4194304 | tf_op jit(solution)/shard_map/all_to_all | solution.py:102
  480.8 1.6 convert_element_type.150
  482.4 0.7 copy-done.2
  483.1 3.0 fusion.20
  486.1 40.5 %all-to-all-done.9 = bf16[32,32,1024]{2,1,0:T(8,128)(2,1)} async-done(((bf16[32,32,1024]{2,1,0:T(8,128)(2,1)}), bf16[32,32,1024]{2,1,0:T(8,128)(2,1)}, u32[]{:S(2)}, u32[]{:S(2)}) %all-to-all-start.9) | async-done | bytes 2097184 | tf_op jit(solution)/shard_map/all_to_all | solution.py:102
  526.6 3.8 multiply_reduce_fusion
  (38 shorter events, 1.7 us)
Async XLA Ops:
  7.2 240.2 %copy-start = (bf16[256,4096]{1,0:T(8,128)(2,1)S(1)}, bf16[256,4096]{1,0:T(8,128)(2,1)}, u32[]{:S(2)}) copy-start(bf16[256,4096]{1,0:T(8,128)(2,1)} %param.10) | copy-start | bytes 6291460
  7.2 38.5 %copy-start.6 = (bf16[1,4096,128]{2,1,0:T(8,128)(2,1)S(1)}, bf16[1,4096,128]{2,1,0:T(8,128)(2,1)}, u32[]{:S(2)}) copy-start(bf16[1,4096,128]{2,1,0:T(8,128)(2,1)} %param.16) | copy-start | bytes 3145732
  7.2 70.0 %copy-start.7 = (bf16[1,4096,128]{2,1,0:T(8,128)(2,1)S(1)}, bf16[1,4096,128]{2,1,0:T(8,128)(2,1)}, u32[]{:S(2)}) copy-start(bf16[1,4096,128]{2,1,0:T(8,128)(2,1)} %param.15) | copy-start | bytes 3145732
  77.2 38.8 %copy-start.10 = (s32[32]{0:T(128)S(1)}, s32[32]{0:T(128)}, u32[]{:S(2)}) copy-start(s32[32]{0:T(128)} %param.13) | copy-start | bytes 388
  108.4 32.0 %all-to-all-start = ((bf16[32,128,128]{2,1,0:T(8,128)(2,1)}), bf16[32,128,128]{2,1,0:T(8,128)(2,1)}, u32[]{:S(2)}, u32[]{:S(2)}) async-start(bf16[32,128,128]{2,1,0:T(8,128)(2,1)} %bitcast), calls=%async_computation | async-start | bytes 2097152 | tf_op jit(solution)/shard_map/all_to_all | solution.py:40
  207.8 36.9 %copy-start.8 = (s32[256,2]{0,1:T(2,128)S(1)}, s32[256,2]{0,1:T(2,128)}, u32[]{:S(2)}) copy-start(s32[256,2]{0,1:T(2,128)} %param.11) | copy-start | bytes 6148
  238.0 29.3 %all-to-all-start.1 = ((bf16[32,128,128]{2,1,0:T(8,128)(2,1)}), bf16[32,128,128]{2,1,0:T(8,128)(2,1)}, u32[]{:S(2)}, u32[]{:S(2)}) async-start(bf16[32,128,128]{2,1,0:T(8,128)(2,1)} %get-tuple-element.13), calls=%async_computation.1 | async-start | bytes 2097152 | tf_op jit(solution)/shard_map/all_to_all | solution.py:55
  267.2 187.4 %all-to-all-start.8 = ((bf16[32,32,4096]{2,1,0:T(8,128)(2,1)}), bf16[32,32,4096]{2,1,0:T(8,128)(2,1)}, u32[]{:S(2)}, u32[]{:S(2)}) async-start(bf16[32,32,4096]{2,1,0:T(8,128)(2,1)} %bitcast.93), calls=%async_computation.8 | async-start | bytes 16777216 | tf_op jit(solution)/shard_map/all_to_all | solution.py:86
  274.9 179.7 %all-gather.2.cloned.1.call-start = ((), (), s32[]{:S(2)}) async-start(), calls=%async_computation.10 | async-start | bytes 9437184 | tf_op jit(solution)/shard_map/all_gather | solution.py:97
  275.1 1.6 copy-start.5
  276.7 1.4 copy-start.1
  278.1 1.3 copy-start.3
  469.9 56.7 %all-to-all-start.9 = ((bf16[32,32,1024]{2,1,0:T(8,128)(2,1)}), bf16[32,32,1024]{2,1,0:T(8,128)(2,1)}, u32[]{:S(2)}, u32[]{:S(2)}) async-start(bf16[32,32,1024]{2,1,0:T(8,128)(2,1)} %bitcast.98), calls=%async_computation.9 | async-start | bytes 4194304 | tf_op jit(solution)/shard_map/all_to_all | solution.py:102
  480.5 1.9 copy-start.4
  480.7 2.4 copy-start.2
  483.1 43.5 %copy-start.9 = (f32[256,2]{0,1:T(2,128)S(1)}, f32[256,2]{0,1:T(2,128)}, u32[]{:S(2)}) copy-start(f32[256,2]{0,1:T(2,128)} %param.12) | copy-start | bytes 6148
Sparse Core Ops, SparseCore 0:
  283.3 62.1 all-gather.1
where the time goes:
time: 542 us; the launch traced here: 537 us
  waiting for transfers between devices  243 us (45%)
  blocking collectives  193 us (36%)
  starting transfers between devices  32.8 us (6%)
  matrix products  24.7 us (5%)
  other arithmetic  15.4 us (3%)
  local copies, waits for them, and re-layouts  14.6 us (3%)
  between operations  14.3 us (3%)
    all_to_all x1, waiting for transfers between devices, shards(): lax.all_to_all(outgoing.reshape(experts, capacity, width), 'expert', spli...  171 us
    all_to_all x1, waiting for transfers between devices, shards(): lax.all_to_all(acts.reshape(experts, capacity, hidden), 'expert', split_a...  40.5 us
    all_to_all x1, blocking collectives, shards(): lax.all_to_all(to_pieces(second_moment[0], experts), 'expert', split_axis...  38.5 us
    all_to_all x1, blocking collectives, shards(): lax.all_to_all(to_pieces(first_moment[0], experts), 'expert', split_axis=...  31.5 us
    all_to_all x1, blocking collectives, shards(): lax.all_to_all(to_pieces(grads[0], experts), 'expert', split_axis=0, conc...  31.2 us
    all_to_all x1, blocking collectives, shards(): lax.all_to_all(chosen[1], 'expert', split_axis=0, concat_axis=0, tiled=True)  31 us
    all_to_all x1, blocking collectives, shards(): lax.all_to_all(chosen[3], 'expert', split_axis=0, concat_axis=0, tiled=True)  30.3 us
    all_to_all x1, blocking collectives, shards(): lax.all_to_all(chosen[2], 'expert', split_axis=0, concat_axis=0, tiled=True)  30.1 us
  transfers between devices with their start and end apart: 5, of which 4 were waited for; matrix products, arithmetic and copies ran while one was open for 5% of the time, Pallas kernels for 0%

commit v1 on v0

v1 whole, which is shorter than its diff:
```python
import jax
import jax.numpy as jnp
from jax import lax
from jax.sharding import Mesh, PartitionSpec as P

beta_one = 0.9
beta_two = 0.999
learn_rate = 0.008
adam_eps = 1e-08

Z_DIM = 8
X_DIM = 4


def adam_step(weight, gradient, first, second):
    grad_wide = gradient.astype(jnp.float32)
    first_wide = beta_one * first.astype(jnp.float32) + (1.0 - beta_one) * grad_wide
    second_wide = beta_two * second.astype(jnp.float32) + (1.0 - beta_two) * grad_wide * grad_wide
    updated = weight.astype(jnp.float32) - learn_rate * first_wide / (
        jnp.sqrt(second_wide) + adam_eps
    )
    return (
        updated.astype(jnp.bfloat16),
        first_wide.astype(jnp.bfloat16),
        second_wide.astype(jnp.bfloat16),
    )


def shards(
    tokens, routes, route_weights, placement, expert_weights, grads, first_moment, second_moment
):
    experts = Z_DIM * X_DIM
    width = tokens.shape[1]
    depth, piece = expert_weights.shape[1:]
    updated, first_low, second_low = adam_step(
        expert_weights[0], grads[0], first_moment[0], second_moment[0]
    )
    tok_count = tokens.shape[0]
    capacity = 4 * tok_count // experts
    expert_ids = jnp.arange(experts, dtype=jnp.int32)
    entries = routes.reshape(2 * tok_count)
    onehot = (entries[:, None] == expert_ids[None, :]).astype(jnp.int32)
    before = jnp.cumsum(onehot, axis=0) - onehot
    position = jnp.sum(before * onehot, axis=1)
    target_slot = entries * capacity + position
    select = (
        target_slot[:, None] == jnp.arange(experts * capacity, dtype=jnp.int32)[None, :]
    ).astype(jnp.bfloat16)
    select_pairs = select.reshape(tok_count, 2, experts * capacity)
    select_tokens = jnp.sum(select_pairs, axis=1)
    outgoing = jnp.einsum(
        "ts,td->sd", select_tokens, tokens, preferred_element_type=jnp.float32
    ).astype(jnp.bfloat16)
    received = lax.all_to_all(
        outgoing.reshape(experts, capacity, width), ("dp", "x"),
        split_axis=0, concat_axis=0, tiled=True,
    )
    slot_rows = received.reshape(experts * capacity, width)
    column = lax.all_gather(updated, "z", axis=0, tiled=False)
    served = lax.all_to_all(column, "dp", split_axis=0, concat_axis=0, tiled=True)
    full = served.transpose(1, 0, 2).reshape(depth, 8 * piece)
    state = jnp.stack(
        [a.reshape(experts, depth // experts, piece) for a in (updated, first_low, second_low)],
        axis=1,
    )
    spread = lax.all_to_all(state, ("z", "x"), split_axis=0, concat_axis=0, tiled=True)
    chosen = jnp.take(spread, placement, axis=0)
    collected = lax.all_to_all(chosen, ("z", "x"), split_axis=0, concat_axis=0, tiled=True)
    acts = jax.nn.silu(
        jnp.dot(slot_rows, full, preferred_element_type=jnp.float32)
    ).astype(jnp.bfloat16)
    hidden = acts.shape[1]
    returned = lax.all_to_all(
        acts.reshape(experts, capacity, hidden), ("dp", "x"), split_axis=0, concat_axis=0, tiled=True
    )
    back_rows = returned.reshape(experts * capacity, hidden)
    picked = jnp.einsum("tks,sh->tkh", select_pairs, back_rows, preferred_element_type=jnp.float32)
    mixed = jnp.sum(route_weights[:, :, None] * picked, axis=1).astype(jnp.bfloat16)
    return tuple(collected[:, i].reshape(1, depth, piece) for i in range(3)) + (mixed,)


def solution(mesh):
    grid = Mesh(mesh.devices.reshape(8, Z_DIM, X_DIM), ("dp", "z", "x"))
    rows = P(("dp", "z", "x"), None)
    state = P(("z", "x"), None, "dp")
    return jax.shard_map(
        shards,
        mesh=grid,
        in_specs=(rows, rows, rows, P(), state, state, state, state),
        out_specs=(state, state, state, rows),
        check_vma=False,
    )
```

time: 542 us -> 468 us (0.86)
  blocking collectives: 193 us -> 0 us
  waiting for transfers between devices: 243 us -> 350 us
  starting transfers between devices: 32.8 us -> 39.4 us
  local copies, waits for them, and re-layouts: 14.6 us -> 20.4 us
    all_to_all x6 -> x0, blocking collectives: 193 us -> none  [the longest x1 38.5 us: shards(): lax.all_to_all(to_pieces(second_moment[0], experts), 'expert', split_axis...]
    all_to_all x4 -> x5, waiting for transfers between devices: 243 us -> 319 us  [the longest x1 98.4 us: shards(): lax.all_to_all(state, ('z', 'x'), split_axis=0, concat_axis=0, tiled=True)]
    all_gather x1, waiting for transfers between devices: 0.01 us -> 30.9 us  [shards(): column = lax.all_gather(updated, 'z', axis=0, tiled=False)]
    all_gather x0 -> x1, local copies, waits for them, and re-layouts: none -> 11.3 us  [shards(): column = lax.all_gather(updated, 'z', axis=0, tiled=False)]
    all_to_all x4 -> x5, starting transfers between devices: 32.6 us -> 39.4 us  [the longest x1 12.1 us: shards(): lax.all_to_all(state, ('z', 'x'), split_axis=0, concat_axis=0, tiled=True)]
    gather x4 -> x1, local copies, waits for them, and re-layouts: 10.6 us -> 4.57 us  [shards(): chosen = jnp.take(spread, placement, axis=0)]
    convert_element_type x1 -> x2, other arithmetic: 3.83 us -> 9.75 us  [adam_step(): updated.astype(jnp.bfloat16)]
  transfers between devices with their start and end apart: 5 -> 6, of which waited for: 4 -> 6; matrix products, arithmetic and copies ran while one was open for 5% -> 11% of each run, Pallas kernels for 0% -> 0%
where the time goes in v1:
time: 468 us; the launch traced here: 467 us
  waiting for transfers between devices  350 us (75%)
  starting transfers between devices  39.4 us (8%)
  matrix products  24.9 us (5%)
  local copies, waits for them, and re-layouts  20.4 us (4%)
  other arithmetic  18.1 us (4%)
  between operations  14.2 us (3%)
    all_to_all x1, waiting for transfers between devices, shards(): lax.all_to_all(state, ('z', 'x'), split_axis=0, concat_axis=0, tiled=True)  98.4 us
    all_to_all x1, waiting for transfers between devices, shards(): lax.all_to_all(column, 'dp', split_axis=0, concat_axis=0, tiled=True)  85.3 us
    all_to_all x1, waiting for transfers between devices, shards(): lax.all_to_all(outgoing.reshape(experts, capacity, width), ('dp', 'x'), s...  56.8 us
    all_to_all x1, waiting for transfers between devices, shards(): lax.all_to_all(chosen, ('z', 'x'), split_axis=0, concat_axis=0, tiled=True)  55.4 us
    all_gather x1, waiting for transfers between devices, shards(): column = lax.all_gather(updated, 'z', axis=0, tiled=False)  30.9 us
    all_to_all x1, waiting for transfers between devices, shards(): lax.all_to_all(acts.reshape(experts, capacity, hidden), ('dp', 'x'), spli...  23.2 us
    dot_general x1, matrix products, shards(): jnp.dot(slot_rows, full, preferred_element_type=jnp.float32)  15.3 us
    all_to_all x1, starting transfers between devices, shards(): lax.all_to_all(state, ('z', 'x'), split_axis=0, concat_axis=0, tiled=True)  12.1 us
  transfers between devices with their start and end apart: 6, of which 6 were waited for; matrix products, arithmetic and copies ran while one was open for 11% of the time, Pallas kernels for 0%

profile of v1, /device:TPU:1, one launch (start us, length us, event | category | flops | bytes accessed | tf_op | source)
XLA Modules:
  0.0 467.0 jit_solution(8642323822296293752)
XLA Ops:
  7.2 0.0 all-gather.2.cloned.1.call-start
  7.2 5.7 %fusion.6 = (bf16[1,4096,128]{2,1,0:T(8,128)(2,1)}, f32[1,4096,128]{2,1,0:T(8,128)}, f32[1,4096,128]{2,1,0:T(8,128)}) fusion(bf16[1,4096,128]{2,1,0:T(8,128)(2,1)} %param.13, bf16[1,4096,128]{2,1,0:T(8,128)(2,1)} %param.12, bf16[1,4096,128]{2,1,0:T(8,128)(2,1)} %param.14, bf16[1,4096,128]{2,1,0:T(8,128)(2,1)} %param.15), kind=kLoop, calls=%fused_computation.20 | loop fusion | flops 8388608 | bytes 9437184 | tf_op jit(solution)/shard_map/convert_element_type | solution.py:23
  13.0 4.0 subtract_convert_fusion
  17.1 0.8 fusion.15
  17.8 2.0 pad_maximum_fusion
  19.8 12.1 %all-to-all-start = ((bf16[32,3,128,128]{3,2,1,0:T(8,128)(2,1)}), bf16[32,3,128,128]{3,2,1,0:T(8,128)(2,1)}, u32[]{:S(2)}, u32[]{:S(2)}) async-start(bf16[32,3,128,128]{3,2,1,0:T(8,128)(2,1)} %pad_maximum_fusion), calls=%async_computation | async-start | bytes 6291456 | tf_op jit(solution)/shard_map/all_to_all | solution.py:66
  31.9 0.1 copy.42
  32.1 0.1 eq.65
  32.2 0.1 eq.61
  32.4 1.2 reduce-window.6
  33.5 0.2 slice_reduce_fusion
  33.8 0.1 fusion.19
  33.9 0.1 reduce_sum.33
  34.1 0.1 copy.45
  34.2 0.3 fusion.13
  34.4 5.6 %convolution_convert_fusion = bf16[1024,4096]{1,0:T(8,128)(2,1)} fusion(bf16[256,1024]{1,0:T(8,128)(2,1)S(1)} %fusion.13, bf16[256,4096]{1,0:T(8,128)(2,1)S(1)} %copy-done), kind=kOutput, calls=%fused_computation.1 | convolution fusion | flops 2151677952 | bytes 11010048 | tf_op jit(solution)/shard_map/ts,td->sd/dot_general | solution.py:51
  40.1 98.4 %all-to-all-done = bf16[32,3,128,128]{3,2,1,0:T(8,128)(2,1)} async-done(((bf16[32,3,128,128]{3,2,1,0:T(8,128)(2,1)}), bf16[32,3,128,128]{3,2,1,0:T(8,128)(2,1)}, u32[]{:S(2)}, u32[]{:S(2)}) %all-to-all-start) | async-done | bytes 3145760 | tf_op jit(solution)/shard_map/all_to_all | solution.py:66
  138.5 9.1 %all-to-all-start.2 = ((bf16[32,32,4096]{2,1,0:T(8,128)(2,1)}), bf16[32,32,4096]{2,1,0:T(8,128)(2,1)}, u32[]{:S(2)}, u32[]{:S(2)}) async-start(bf16[32,32,4096]{2,1,0:T(8,128)(2,1)} %bitcast.47), calls=%async_computation.2 | async-start | bytes 16777216 | tf_op jit(solution)/shard_map/all_to_all | solution.py:54
  147.6 30.9 %all-gather.2.cloned.1.call-done = bf16[8,4096,128]{2,1,0:T(8,128)(2,1)} async-done(((bf16[1,4096,128]{2,1,0:T(8,128)(2,1)}), bf16[8,4096,128]{2,1,0:T(8,128)(2,1)}) %all-gather.2.cloned.1.call-update) | async-done | bytes 8388624 | tf_op jit(solution)/shard_map/all_gather | solution.py:59
  178.5 11.3 %copy.46 = bf16[8,4096,128]{1,2,0:T(8,128)(2,1)} copy(bf16[8,4096,128]{2,1,0:T(8,128)(2,1)} %all-gather.2.cloned.1.call-done) | data formatting | bytes 16777216 | tf_op jit(solution)/shard_map/all_gather | solution.py:59
  189.8 56.8 %all-to-all-done.2 = bf16[32,32,4096]{2,1,0:T(8,128)(2,1)} async-done(((bf16[32,32,4096]{2,1,0:T(8,128)(2,1)}), bf16[32,32,4096]{2,1,0:T(8,128)(2,1)}, u32[]{:S(2)}, u32[]{:S(2)}) %all-to-all-start.2) | async-done | bytes 8388640 | tf_op jit(solution)/shard_map/all_to_all | solution.py:54
  246.6 5.0 %all-to-all-start.3 = ((bf16[8,4096,128]{1,2,0:T(8,128)(2,1)}), bf16[8,4096,128]{1,2,0:T(8,128)(2,1)}, u32[]{:S(2)}, u32[]{:S(2)}) async-start(bf16[8,4096,128]{1,2,0:T(8,128)(2,1)} %copy.46), calls=%async_computation.3 | async-start | bytes 16777216 | tf_op jit(solution)/shard_map/all_to_all | solution.py:60
  251.6 4.6 gather_fusion
  256.2 4.0 broadcast_select_fusion
  260.1 85.3 %all-to-all-done.3 = bf16[8,4096,128]{1,2,0:T(8,128)(2,1)} async-done(((bf16[8,4096,128]{1,2,0:T(8,128)(2,1)}), bf16[8,4096,128]{1,2,0:T(8,128)(2,1)}, u32[]{:S(2)}, u32[]{:S(2)}) %all-to-all-start.3) | async-done | bytes 8388640 | tf_op jit(solution)/shard_map/all_to_all | solution.py:60
  345.4 5.0 %all-to-all-start.1 = ((bf16[32,3,128,128]{3,2,1,0:T(8,128)(2,1)}), bf16[32,3,128,128]{3,2,1,0:T(8,128)(2,1)}, u32[]{:S(2)}, u32[]{:S(2)}) async-start(bf16[32,3,128,128]{3,2,1,0:T(8,128)(2,1)} %broadcast_select_fusion), calls=%async_computation.1 | async-start | bytes 6291456 | tf_op jit(solution)/shard_map/all_to_all | solution.py:68
  350.4 15.3 %multiply_convert_fusion = bf16[1024,1024]{1,0:T(8,128)(2,1)} fusion(bf16[1024,4096]{1,0:T(8,128)(2,1)} %bitcast.10, bf16[4096,1024]{0,1:T(8,128)(2,1)} %bitcast.12), kind=kOutput, calls=%fused_computation.2 | convolution fusion | flops 8595177472 | bytes 18874368 | tf_op jit(solution)/shard_map/dot_general | solution.py:70
  365.7 55.4 %all-to-all-done.1 = bf16[32,3,128,128]{3,2,1,0:T(8,128)(2,1)} async-done(((bf16[32,3,128,128]{3,2,1,0:T(8,128)(2,1)}), bf16[32,3,128,128]{3,2,1,0:T(8,128)(2,1)}, u32[]{:S(2)}, u32[]{:S(2)}) %all-to-all-start.1) | async-done | bytes 3145760 | tf_op jit(solution)/shard_map/all_to_all | solution.py:68
  421.1 8.2 %all-to-all-start.4 = ((bf16[32,32,1024]{2,1,0:T(8,128)(2,1)}), bf16[32,32,1024]{2,1,0:T(8,128)(2,1)}, u32[]{:S(2)}, u32[]{:S(2)}) async-start(bf16[32,32,1024]{2,1,0:T(8,128)(2,1)} %bitcast.13), calls=%async_computation.4 | async-start | bytes 4194304 | tf_op jit(solution)/shard_map/all_to_all | solution.py:73
  429.3 3.6 fusion.21
  433.0 23.2 %all-to-all-done.4 = bf16[32,32,1024]{2,1,0:T(8,128)(2,1)} async-done(((bf16[32,32,1024]{2,1,0:T(8,128)(2,1)}), bf16[32,32,1024]{2,1,0:T(8,128)(2,1)}, u32[]{:S(2)}, u32[]{:S(2)}) %all-to-all-start.4) | async-done | bytes 2097184 | tf_op jit(solution)/shard_map/all_to_all | solution.py:73
  456.2 4.0 multiply_reduce_fusion
  (24 shorter events, 0.1 us)
Async XLA Ops:
  7.2 27.3 %copy-start = (bf16[256,4096]{1,0:T(8,128)(2,1)S(1)}, bf16[256,4096]{1,0:T(8,128)(2,1)}, u32[]{:S(2)}) copy-start(bf16[256,4096]{1,0:T(8,128)(2,1)} %param.8) | copy-start | bytes 6291460
  7.2 5.8 %copy-start.4 = (bf16[1,4096,128]{2,1,0:T(8,128)(2,1)S(1)}, bf16[1,4096,128]{2,1,0:T(8,128)(2,1)}, u32[]{:S(2)}) copy-start(bf16[1,4096,128]{2,1,0:T(8,128)(2,1)} %param.13) | copy-start | bytes 3145732
  7.2 171.3 %all-gather.2.cloned.1.call-start = ((), (), s32[]{:S(2)}) async-start(), calls=%async_computation.5 | async-start | bytes 9437184 | tf_op jit(solution)/shard_map/all_gather | solution.py:59
  13.0 4.0 copy-start.2
  13.0 4.0 copy-start.3
  19.8 12.1 %copy-start.5 = (s32[256,2]{0,1:T(2,128)S(1)}, s32[256,2]{0,1:T(2,128)}, u32[]{:S(2)}) copy-start(s32[256,2]{0,1:T(2,128)} %param.9) | copy-start | bytes 6148
  19.8 118.7 %all-to-all-start = ((bf16[32,3,128,128]{3,2,1,0:T(8,128)(2,1)}), bf16[32,3,128,128]{3,2,1,0:T(8,128)(2,1)}, u32[]{:S(2)}, u32[]{:S(2)}) async-start(bf16[32,3,128,128]{3,2,1,0:T(8,128)(2,1)} %pad_maximum_fusion), calls=%async_computation | async-start | bytes 6291456 | tf_op jit(solution)/shard_map/all_to_all | solution.py:66
  138.5 108.1 %all-to-all-start.2 = ((bf16[32,32,4096]{2,1,0:T(8,128)(2,1)}), bf16[32,32,4096]{2,1,0:T(8,128)(2,1)}, u32[]{:S(2)}, u32[]{:S(2)}) async-start(bf16[32,32,4096]{2,1,0:T(8,128)(2,1)} %bitcast.47), calls=%async_computation.2 | async-start | bytes 16777216 | tf_op jit(solution)/shard_map/all_to_all | solution.py:54
  189.8 61.8 %copy-start.7 = (s32[32]{0:T(128)S(1)}, s32[32]{0:T(128)}, u32[]{:S(2)}) copy-start(s32[32]{0:T(128)} %param.11) | copy-start | bytes 388
  246.6 98.9 %all-to-all-start.3 = ((bf16[8,4096,128]{1,2,0:T(8,128)(2,1)}), bf16[8,4096,128]{1,2,0:T(8,128)(2,1)}, u32[]{:S(2)}, u32[]{:S(2)}) async-start(bf16[8,4096,128]{1,2,0:T(8,128)(2,1)} %copy.46), calls=%async_computation.3 | async-start | bytes 16777216 | tf_op jit(solution)/shard_map/all_to_all | solution.py:60
  345.4 75.7 %all-to-all-start.1 = ((bf16[32,3,128,128]{3,2,1,0:T(8,128)(2,1)}), bf16[32,3,128,128]{3,2,1,0:T(8,128)(2,1)}, u32[]{:S(2)}, u32[]{:S(2)}) async-start(bf16[32,3,128,128]{3,2,1,0:T(8,128)(2,1)} %broadcast_select_fusion), calls=%async_computation.1 | async-start | bytes 6291456 | tf_op jit(solution)/shard_map/all_to_all | solution.py:68
  421.1 35.1 %all-to-all-start.4 = ((bf16[32,32,1024]{2,1,0:T(8,128)(2,1)}), bf16[32,32,1024]{2,1,0:T(8,128)(2,1)}, u32[]{:S(2)}, u32[]{:S(2)}) async-start(bf16[32,32,1024]{2,1,0:T(8,128)(2,1)} %bitcast.13), calls=%async_computation.4 | async-start | bytes 4194304 | tf_op jit(solution)/shard_map/all_to_all | solution.py:73
  429.3 26.9 %copy-start.6 = (f32[256,2]{0,1:T(2,128)S(1)}, f32[256,2]{0,1:T(2,128)}, u32[]{:S(2)}) copy-start(f32[256,2]{0,1:T(2,128)} %param.10) | copy-start | bytes 6148
  456.2 4.0 copy-start.1
Sparse Core Ops, SparseCore 0:
  13.1 165.3 all-gather.1

commit v2 on v1

v2 whole, which is shorter than its diff:
```python
import jax
import jax.numpy as jnp
from jax import lax
from jax.experimental import pallas as pl
from jax.experimental.pallas import tpu as pltpu
from jax.sharding import PartitionSpec as P

beta_one = 0.9
beta_two = 0.999
learn_rate = 0.008
adam_eps = 1e-08

DP = 8
Z_DIM = 8
X_DIM = 4
EXPERTS = Z_DIM * X_DIM
MESH = pl.DeviceIdType.MESH


def kernel(
    placement_ref, routes_ref, routes_t_ref, weights_ref, tokens_ref, w_ref, g_ref, m_ref, v_ref,
    mixed_ref, final_ref,
    column, served, outgoing, slots, acts, back, spread, landed, chosen,
    ring_send, ring_recv, serve_send, serve_recv, serve_local,
    tok_send, tok_recv, ret_send, ret_recv, one_send, one_recv, two_send, two_recv, two_local,
):
    dp = lax.axis_index("dp")
    own = lax.axis_index("expert")
    z, x = own // X_DIM, own % X_DIM
    mine = dp * X_DIM + x
    cap = slots.shape[0] // EXPERTS
    block = spread.shape[1] // 3
    half = column.shape[1] // 2

    def plane_peer(p):
        return (p // X_DIM, z * X_DIM + p % X_DIM)

    def slot_rows(p):
        return pl.ds(pl.multiple_of(p * cap, cap), cap)

    barrier = pltpu.get_barrier_semaphore()

    @pl.loop(1, EXPERTS)
    def _(o):
        pl.semaphore_signal(
            barrier, inc=1, device_id=plane_peer((mine + o) % EXPERTS), device_id_type=MESH
        )
        pl.semaphore_signal(
            barrier, inc=1, device_id=(dp, (own + o) % EXPERTS), device_id_type=MESH
        )

    @pl.loop(0, EXPERTS)
    def _(j):
        rows = pl.ds(pl.multiple_of(j * block, block), block)
        grad = g_ref[rows, :].astype(jnp.float32)
        first = beta_one * m_ref[rows, :].astype(jnp.float32) + (1.0 - beta_one) * grad
        second = beta_two * v_ref[rows, :].astype(jnp.float32) + (1.0 - beta_two) * grad * grad
        updated = w_ref[rows, :].astype(jnp.float32) - learn_rate * first / (
            jnp.sqrt(second) + adam_eps
        )
        updated = updated.astype(jnp.bfloat16)
        column[z, rows, :] = updated
        spread[j, 0:block, :] = updated
        spread[j, block : 2 * block, :] = first.astype(jnp.bfloat16)
        spread[j, 2 * block : 3 * block, :] = second.astype(jnp.bfloat16)

    landed[own] = spread[own]
    pl.semaphore_wait(barrier, 2 * (EXPERTS - 1))

    def part(ref, at, h):
        return ref.at[at, pl.ds(h * half, half), :]

    def ring_copy(way, step, h, source):
        to = (z + (1 if way == 0 else Z_DIM - 1)) % Z_DIM
        return pltpu.make_async_remote_copy(
            src_ref=part(column, source, h),
            dst_ref=part(column, source, h),
            send_sem=ring_send.at[way, step, h],
            recv_sem=ring_recv.at[way, step, h],
            device_id=(dp, to * X_DIM + x),
            device_id_type=MESH,
        )

    def ring_steps(way, step):
        if step < 3:
            return (0, 1)
        return (way,)

    def ring_source(way, step):
        return (z + (Z_DIM - step if way == 0 else step)) % Z_DIM

    def serve_copy(source, h, sender, target):
        return pltpu.make_async_remote_copy(
            src_ref=part(column, source, h),
            dst_ref=part(served, sender, h),
            send_sem=serve_send.at[source, h],
            recv_sem=serve_recv.at[sender, h],
            device_id=(target, own),
            device_id_type=MESH,
        )

    def serve_own(h):
        return pltpu.make_async_copy(part(column, dp, h), part(served, dp, h), serve_local.at[h])

    def serve(source, h):
        @pl.when(source != dp)
        def _():
            serve_copy(source, h, dp, source).start()

        @pl.when(source == dp)
        def _():
            serve_own(h).start()

    def ring_hop(step):
        for h in (0, 1):
            for way in (0, 1):
                if h not in ring_steps(way, step):
                    continue
                source = ring_source(way, step + 1)
                ring_copy(way, step, h, source).wait_recv()
                if step < 3 and h in ring_steps(way, step + 1):
                    ring_copy(way, step + 1, h, source).start()
                serve(source, h)

    for h in (0, 1):
        for way in (0, 1):
            ring_copy(way, 0, h, z).start()
    for h in (0, 1):
        serve(z, h)

    tok_count = tokens_ref.shape[0]

    def tok_copy(p, sender):
        return pltpu.make_async_remote_copy(
            src_ref=outgoing.at[slot_rows(p), :],
            dst_ref=slots.at[slot_rows(sender), :],
            send_sem=tok_send.at[p],
            recv_sem=tok_recv.at[sender],
            device_id=plane_peer(p),
            device_id_type=MESH,
        )

    named = routes_t_ref[...]
    ids = lax.broadcasted_iota(jnp.int32, (EXPERTS, tok_count), 0)
    hits = [ids == named[k : k + 1, :] for k in (0, 1)]
    both = jnp.where(hits[0] | hits[1], 1.0, 0.0).astype(jnp.bfloat16)
    row = lax.broadcasted_iota(jnp.int32, (tok_count, tok_count), 0)
    col = lax.broadcasted_iota(jnp.int32, (tok_count, tok_count), 1)
    earlier = jnp.where(row < col, 1.0, 0.0).astype(jnp.bfloat16)
    before = jnp.dot(both, earlier, preferred_element_type=jnp.float32)
    wide = [
        named[k : k + 1, :].astype(jnp.float32) * cap
        + jnp.sum(jnp.where(hits[k], before, 0.0), axis=0, keepdims=True)
        for k in (0, 1)
    ]
    group = 8 * cap
    width = tokens_ref.shape[1]
    chunk = 1024

    @pl.loop(0, 4)
    def _(q):
        first_row = ((dp // 2 + q) % 4) * group
        slot_id = (first_row + lax.broadcasted_iota(jnp.int32, (group, tok_count), 0)).astype(
            jnp.float32
        )
        pick = jnp.where((slot_id == wide[0]) | (slot_id == wide[1]), 1.0, 0.0).astype(jnp.bfloat16)
        for c in range(width // chunk):
            outgoing[pl.ds(pl.multiple_of(first_row, group), group), c * chunk : (c + 1) * chunk] = (
                jnp.dot(
                    pick,
                    tokens_ref[:, c * chunk : (c + 1) * chunk],
                    preferred_element_type=jnp.float32,
                ).astype(jnp.bfloat16)
            )

        @pl.loop(0, 8)
        def _(i):
            p = ((dp // 2 + q) % 4) * 8 + (mine + i) % 8

            @pl.when(p != mine)
            def _():
                tok_copy(p, mine).start()

            @pl.when(p == mine)
            def _():
                slots[slot_rows(mine), :] = outgoing[slot_rows(mine), :]

    def one_copy(j, sender):
        return pltpu.make_async_remote_copy(
            src_ref=spread.at[j],
            dst_ref=landed.at[sender],
            send_sem=one_send.at[j],
            recv_sem=one_recv.at[sender],
            device_id=(dp, j),
            device_id_type=MESH,
        )

    def two_copy(j, sender):
        return pltpu.make_async_remote_copy(
            src_ref=chosen.at[j],
            dst_ref=final_ref.at[sender],
            send_sem=two_send.at[j],
            recv_sem=two_recv.at[sender],
            device_id=(dp, j),
            device_id_type=MESH,
        )

    two_own = pltpu.make_async_copy(chosen.at[own], final_ref.at[own], two_local)

    ring_hop(0)
    ring_hop(1)

    @pl.loop(1, EXPERTS)
    def _(o):
        one_copy((own + o) % EXPERTS, own).start()

    ring_hop(2)
    ring_hop(3)

    @pl.loop(0, DP)
    def _(s):
        @pl.when(s != dp)
        def _():
            for h in (0, 1):
                serve_copy(dp, h, s, s).wait_recv()

        @pl.when(s == dp)
        def _():
            for h in (0, 1):
                serve_own(h).wait()

    def ret_copy(p, sender):
        return pltpu.make_async_remote_copy(
            src_ref=acts.at[slot_rows(p), :],
            dst_ref=back.at[slot_rows(sender), :],
            send_sem=ret_send.at[p],
            recv_sem=ret_recv.at[sender],
            device_id=plane_peer(p),
            device_id_type=MESH,
        )

    @pl.loop(0, 4)
    def _(q):
        base = ((dp // 2 + q) % 4) * 8
        rows = pl.ds(pl.multiple_of(base * cap, group), group)

        @pl.loop(0, 8)
        def _(i):
            p = base + i

            @pl.when(p != mine)
            def _():
                tok_copy(p, p).wait_recv()

        @pl.loop(0, DP // 2)
        def _(n):
            right = jnp.concatenate([served[2 * n], served[2 * n + 1]], axis=1)
            total = jnp.dot(slots[rows, :], right, preferred_element_type=jnp.float32)
            acts[rows, pl.ds(pl.multiple_of(n * 256, 256), 256)] = (
                total / (1.0 + jnp.exp(-total))
            ).astype(jnp.bfloat16)

        @pl.loop(0, 8)
        def _(i):
            p = base + (mine + i) % 8

            @pl.when(p != mine)
            def _():
                ret_copy(p, mine).start()

            @pl.when(p == mine)
            def _():
                back[slot_rows(mine), :] = acts[slot_rows(mine), :]

    @pl.loop(1, EXPERTS)
    def _(o):
        p = (own + EXPERTS - o) % EXPERTS
        one_copy(p, p).wait_recv()

    @pl.loop(0, EXPERTS)
    def _(j):
        chosen[j] = landed[placement_ref[j]]

    @pl.loop(1, EXPERTS)
    def _(o):
        two_copy((own + o) % EXPERTS, own).start()

    two_own.start()

    tall_named = routes_ref[...]
    lanes = lax.broadcasted_iota(jnp.int32, (tok_count, EXPERTS), 1)
    tall_hits = [lanes == tall_named[:, k : k + 1] for k in (0, 1)]
    tall_both = jnp.where(tall_hits[0] | tall_hits[1], 1.0, 0.0).astype(jnp.bfloat16)
    later = jnp.where(col < row, 1.0, 0.0).astype(jnp.bfloat16)
    tall_before = jnp.dot(later, tall_both, preferred_element_type=jnp.float32)
    slot_lane = lax.broadcasted_iota(jnp.int32, (tok_count, EXPERTS * cap), 1).astype(jnp.float32)
    tall_pick = []
    for k in (0, 1):
        slot = tall_named[:, k : k + 1].astype(jnp.float32) * cap + jnp.sum(
            jnp.where(tall_hits[k], tall_before, 0.0), axis=1, keepdims=True
        )
        tall_pick.append(jnp.where(slot_lane == slot, 1.0, 0.0).astype(jnp.bfloat16))

    @pl.loop(1, EXPERTS)
    def _(o):
        p = (mine + EXPERTS - o) % EXPERTS
        ret_copy(p, p).wait_recv()

    gain = weights_ref[...]
    for c in range(2):
        cols = slice(c * 512, (c + 1) * 512)
        got = [
            jnp.dot(tall_pick[k], back[:, cols], preferred_element_type=jnp.float32) for k in (0, 1)
        ]
        mixed_ref[:, cols] = (gain[:, 0:1] * got[0] + gain[:, 1:2] * got[1]).astype(jnp.bfloat16)

    @pl.loop(1, EXPERTS)
    def _(o):
        p = (mine + o) % EXPERTS
        tok_copy(p, mine).wait_send()
        ret_copy(p, mine).wait_send()
        j = (own + o) % EXPERTS
        one_copy(j, own).wait_send()
        two_copy(j, own).wait_send()

    for step in range(4):
        for way in (0, 1):
            for h in ring_steps(way, step):
                ring_copy(way, step, h, ring_source(way, step)).wait_send()

    @pl.loop(0, Z_DIM)
    def _(s):
        @pl.when(s != dp)
        def _():
            for h in (0, 1):
                serve_copy(s, h, dp, s).wait_send()

    @pl.loop(1, EXPERTS)
    def _(o):
        p = (own + EXPERTS - o) % EXPERTS
        two_copy(p, p).wait_recv()

    two_own.wait()


def shards(
    tokens, routes, route_weights, placement, expert_weights, grads, first_moment, second_moment
):
    depth, piece = expert_weights.shape[1:]
    count, width = tokens.shape
    hidden = DP * piece
    cap = 4 * count // EXPERTS
    block = depth // EXPERTS
    vmem = pl.BlockSpec(memory_space=pltpu.VMEM)
    dma = pltpu.SemaphoreType.DMA
    mixed, final = pl.pallas_call(
        kernel,
        out_shape=(
            jax.ShapeDtypeStruct((count, hidden), jnp.bfloat16),
            jax.ShapeDtypeStruct((EXPERTS, 3 * block, piece), jnp.bfloat16),
        ),
        in_specs=[pl.BlockSpec(memory_space=pltpu.SMEM)] + [vmem] * 8,
        out_specs=(vmem, pl.BlockSpec(memory_space=pl.ANY)),
        scratch_shapes=[
            pltpu.VMEM((Z_DIM, depth, piece), jnp.bfloat16),
            pltpu.VMEM((DP, depth, piece), jnp.bfloat16),
            pltpu.VMEM((EXPERTS * cap, width), jnp.bfloat16),
            pltpu.VMEM((EXPERTS * cap, width), jnp.bfloat16),
            pltpu.VMEM((EXPERTS * cap, hidden), jnp.bfloat16),
            pltpu.VMEM((EXPERTS * cap, hidden), jnp.bfloat16),
            pltpu.VMEM((EXPERTS, 3 * block, piece), jnp.bfloat16),
            pltpu.VMEM((EXPERTS, 3 * block, piece), jnp.bfloat16),
            pltpu.VMEM((EXPERTS, 3 * block, piece), jnp.bfloat16),
            dma((2, 4, 2)),
            dma((2, 4, 2)),
            dma((Z_DIM, 2)),
            dma((DP, 2)),
            dma((2,)),
        ]
        + [dma((EXPERTS,))] * 8
        + [dma],
        compiler_params=pltpu.CompilerParams(
            collective_id=0, has_side_effects=True, vmem_limit_bytes=60 * 1024 * 1024
        ),
    )(
        placement, routes, routes.T, route_weights, tokens,
        expert_weights[0], grads[0], first_moment[0], second_moment[0],
    )
    state = final.reshape(EXPERTS, 3, block, piece)
    return tuple(state[:, i].reshape(1, depth, piece) for i in range(3)) + (mixed,)


def solution(mesh):
    rows = P(("dp", "expert"), None)
    state = P("expert", None, "dp")
    return jax.shard_map(
        shards,
        mesh=mesh,
        in_specs=(rows, rows, rows, P(), state, state, state, state),
        out_specs=(state, state, state, rows),
        check_vma=False,
    )
```

time: 468 us -> 308 us (0.66)
  the two profiles are of different devices: /device:TPU:1 before, /device:TPU:79 now
where the time goes in v2:
time: 308 us
  Pallas kernels  300 us (97%)
  local copies, waits for them, and re-layouts  7.45 us (2%)
    pallas_call x1, Pallas kernels, shards(): pl.pallas_call(kernel, out_shape=(jax.ShapeDtypeStruct((count, hidden), j...  300 us

profile of v2, /device:TPU:79, one launch (start us, length us, event | category | flops | bytes accessed | tf_op | source)
XLA Modules:
  0.0 307.9 jit_solution(9692169876251288655)
XLA Ops:
  0.6 1.5 copy.13.weights_ref
  2.1 1.5 copy.12.routes_ref
  3.6 299.8 %shard_map.111 = (bf16[256,1024]{1,0:T(8,128)(2,1)}, bf16[32,384,128]{2,1,0:T(8,128)(2,1)}) custom-call(s32[32]{0:T(128)} %placement_ref.1, s32[256,2]{1,0:T(8,128)} %copy.12.routes_ref, s32[2,256]{1,0:T(2,128)} %bitcast.17, f32[256,2]{1,0:T(8,128)} %copy.13.weights_ref, bf16[256,4096]{1,0:T(8,128)(2,1)} %tokens_ref.1, bf16[4096,128]{1,0:T(8,128)(2,1)} %bitcast.10, ...), custom_call_target="tpu_custom_call" | custom-call | tf_op jit(solution)/shard_map/pallas_call | solution.py:356
  303.4 0.0 copy-start
  303.4 3.7 %fusion = (bf16[32,1,128,128]{3,2,1,0:T(8,128)(2,1)}, bf16[32,1,128,128]{3,2,1,0:T(8,128)(2,1)}, bf16[32,1,128,128]{3,2,1,0:T(8,128)(2,1)}) fusion(bf16[32,3,128,128]{3,2,1,0:T(8,128)(2,1)} %bitcast.9), kind=kLoop, calls=%fused_computation | loop fusion | bytes 6291456 | tf_op jit(solution)/shard_map/slice | solution.py:390
  307.1 0.0 copy-done
  307.1 0.8 copy.15
Async XLA Ops:
  303.4 3.7 %copy-start = (bf16[256,1024]{1,0:T(8,128)(2,1)S(1)}, bf16[256,1024]{1,0:T(8,128)(2,1)}, u32[]{:S(2)}) copy-start(bf16[256,1024]{1,0:T(8,128)(2,1)} %get-tuple-element.18) | copy-start | bytes 1572868

commit v3 on v2

--- a/solution.py
+++ b/solution.py
@@ -14,6 +14,7 @@
 Z_DIM = 8
 X_DIM = 4
 EXPERTS = Z_DIM * X_DIM
+WAVES = 8
 MESH = pl.DeviceIdType.MESH
 
 
@@ -30,7 +31,7 @@
     mine = dp * X_DIM + x
     cap = slots.shape[0] // EXPERTS
     block = spread.shape[1] // 3
-    half = column.shape[1] // 2
+    part_rows = column.shape[1] // WAVES
 
     def plane_peer(p):
         return (p // X_DIM, z * X_DIM + p % X_DIM)
@@ -68,7 +69,7 @@
     pl.semaphore_wait(barrier, 2 * (EXPERTS - 1))
 
     def part(ref, at, h):
-        return ref.at[at, pl.ds(h * half, half), :]
+        return ref.at[at, pl.ds(pl.multiple_of(h * part_rows, part_rows), part_rows), :]
 
     def ring_copy(way, step, h, source):
         to = (z + (1 if way == 0 else Z_DIM - 1)) % Z_DIM
@@ -81,11 +82,6 @@
             device_id_type=MESH,
         )
 
-    def ring_steps(way, step):
-        if step < 3:
-            return (0, 1)
-        return (way,)
-
     def ring_source(way, step):
         return (z + (Z_DIM - step if way == 0 else step)) % Z_DIM
 
@@ -111,22 +107,38 @@
         def _():
             serve_own(h).start()
 
-    def ring_hop(step):
-        for h in (0, 1):
-            for way in (0, 1):
-                if h not in ring_steps(way, step):
-                    continue
-                source = ring_source(way, step + 1)
-                ring_copy(way, step, h, source).wait_recv()
-                if step < 3 and h in ring_steps(way, step + 1):
-                    ring_copy(way, step + 1, h, source).start()
-                serve(source, h)
-
-    for h in (0, 1):
+    def ring_start(h):
         for way in (0, 1):
             ring_copy(way, 0, h, z).start()
-    for h in (0, 1):
         serve(z, h)
+
+    def ring_hop(step, h, parity):
+        for way in (0, 1):
+            if step == 3 and way != parity:
+                continue
+            source = ring_source(way, step + 1)
+            ring_copy(way, step, h, source).wait_recv()
+            if step < 2 or (step == 2 and way == parity):
+                ring_copy(way, step + 1, h, source).start()
+            serve(source, h)
+
+    def ring_waves(first, last):
+        @pl.loop(first, last)
+        def _(v):
+            for step in range(3):
+                for parity in (0, 1):
+                    ring_hop(step, 2 * v + parity, parity)
+
+            @pl.when(v < WAVES // 2 - 1)
+            def _():
+                for parity in (0, 1):
+                    ring_start(2 * v + 2 + parity)
+
+            for parity in (0, 1):
+                ring_hop(3, 2 * v + parity, parity)
+
+    for parity in (0, 1):
+        ring_start(parity)
 
     tok_count = tokens_ref.shape[0]
 
@@ -207,26 +219,41 @@
 
     two_own = pltpu.make_async_copy(chosen.at[own], final_ref.at[own], two_local)
 
-    ring_hop(0)
-    ring_hop(1)
+    ring_waves(0, WAVES // 4)
 
     @pl.loop(1, EXPERTS)
     def _(o):
         one_copy((own + o) % EXPERTS, own).start()
 
-    ring_hop(2)
-    ring_hop(3)
+    ring_waves(WAVES // 4, WAVES // 2)
+
+    @pl.loop(1, EXPERTS)
+    def _(o):
+        p = (own + EXPERTS - o) % EXPERTS
+        one_copy(p, p).wait_recv()
+
+    @pl.loop(0, EXPERTS)
+    def _(j):
+        chosen[j] = landed[placement_ref[j]]
+
+    @pl.loop(1, EXPERTS)
+    def _(o):
+        two_copy((own + o) % EXPERTS, own).start()
+
+    two_own.start()
 
     @pl.loop(0, DP)
     def _(s):
         @pl.when(s != dp)
         def _():
-            for h in (0, 1):
+            @pl.loop(0, WAVES)
+            def _(h):
                 serve_copy(dp, h, s, s).wait_recv()
 
         @pl.when(s == dp)
         def _():
-            for h in (0, 1):
+            @pl.loop(0, WAVES)
+            def _(h):
                 serve_own(h).wait()
 
     def ret_copy(p, sender):
@@ -271,21 +298,6 @@
             @pl.when(p == mine)
             def _():
                 back[slot_rows(mine), :] = acts[slot_rows(mine), :]
-
-    @pl.loop(1, EXPERTS)
-    def _(o):
-        p = (own + EXPERTS - o) % EXPERTS
-        one_copy(p, p).wait_recv()
-
-    @pl.loop(0, EXPERTS)
-    def _(j):
-        chosen[j] = landed[placement_ref[j]]
-
-    @pl.loop(1, EXPERTS)
-    def _(o):
-        two_copy((own + o) % EXPERTS, own).start()
-
-    two_own.start()
 
     tall_named = routes_ref[...]
     lanes = lax.broadcasted_iota(jnp.int32, (tok_count, EXPERTS), 1)
@@ -323,16 +335,20 @@
         one_copy(j, own).wait_send()
         two_copy(j, own).wait_send()
 
-    for step in range(4):
-        for way in (0, 1):
-            for h in ring_steps(way, step):
-                ring_copy(way, step, h, ring_source(way, step)).wait_send()
+    @pl.loop(0, WAVES // 2)
+    def _(v):
+        for parity in (0, 1):
+            for step in range(4):
+                for way in (0, 1):
+                    if step < 3 or way == parity:
+                        ring_copy(way, step, 2 * v + parity, ring_source(way, step)).wait_send()
 
     @pl.loop(0, Z_DIM)
     def _(s):
         @pl.when(s != dp)
         def _():
-            for h in (0, 1):
+            @pl.loop(0, WAVES)
+            def _(h):
                 serve_copy(s, h, dp, s).wait_send()
 
     @pl.loop(1, EXPERTS)
@@ -371,11 +387,11 @@
             pltpu.VMEM((EXPERTS, 3 * block, piece), jnp.bfloat16),
             pltpu.VMEM((EXPERTS, 3 * block, piece), jnp.bfloat16),
             pltpu.VMEM((EXPERTS, 3 * block, piece), jnp.bfloat16),
-            dma((2, 4, 2)),
-            dma((2, 4, 2)),
-            dma((Z_DIM, 2)),
-            dma((DP, 2)),
-            dma((2,)),
+            dma((2, 4, WAVES)),
+            dma((2, 4, WAVES)),
+            dma((Z_DIM, WAVES)),
+            dma((DP, WAVES)),
+            dma((WAVES,)),
         ]
         + [dma((EXPERTS,))] * 8
         + [dma],

time: 308 us -> 262 us (0.85)
  the two profiles are of different devices: /device:TPU:79 before, /device:TPU:1 now
where the time goes in v3:
time: 262 us
  Pallas kernels  254 us (97%)
  local copies, waits for them, and re-layouts  7.45 us (3%)
    pallas_call x1, Pallas kernels, shards(): pl.pallas_call(kernel, out_shape=(jax.ShapeDtypeStruct((count, hidden), j...  254 us

profile of v3, /device:TPU:1, one launch (start us, length us, event | category | flops | bytes accessed | tf_op | source)
XLA Modules:
  0.0 262.0 jit_solution(17298630358088662897)
XLA Ops:
  0.6 1.5 copy.13.weights_ref
  2.1 1.5 copy.12.routes_ref
  3.6 253.9 %shard_map.111 = (bf16[256,1024]{1,0:T(8,128)(2,1)}, bf16[32,384,128]{2,1,0:T(8,128)(2,1)}) custom-call(s32[32]{0:T(128)} %placement_ref.1, s32[256,2]{1,0:T(8,128)} %copy.12.routes_ref, s32[2,256]{1,0:T(2,128)} %bitcast.17, f32[256,2]{1,0:T(8,128)} %copy.13.weights_ref, bf16[256,4096]{1,0:T(8,128)(2,1)} %tokens_ref.1, bf16[4096,128]{1,0:T(8,128)(2,1)} %bitcast.10, ...), custom_call_target="tpu_custom_call" | custom-call | tf_op jit(solution)/shard_map/pallas_call | solution.py:372
  257.5 0.0 copy-start
  257.5 3.7 %fusion = (bf16[32,1,128,128]{3,2,1,0:T(8,128)(2,1)}, bf16[32,1,128,128]{3,2,1,0:T(8,128)(2,1)}, bf16[32,1,128,128]{3,2,1,0:T(8,128)(2,1)}) fusion(bf16[32,3,128,128]{3,2,1,0:T(8,128)(2,1)} %bitcast.9), kind=kLoop, calls=%fused_computation | loop fusion | bytes 6291456 | tf_op jit(solution)/shard_map/slice | solution.py:406
  261.2 0.0 copy-done
  261.2 0.8 copy.15
Async XLA Ops:
  257.5 3.7 %copy-start = (bf16[256,1024]{1,0:T(8,128)(2,1)S(1)}, bf16[256,1024]{1,0:T(8,128)(2,1)}, u32[]{:S(2)}) copy-start(bf16[256,1024]{1,0:T(8,128)(2,1)} %get-tuple-element.18) | copy-start | bytes 1572868

commit v4 on v3

--- a/solution.py
+++ b/solution.py
@@ -14,16 +14,18 @@
 Z_DIM = 8
 X_DIM = 4
 EXPERTS = Z_DIM * X_DIM
-WAVES = 8
+WAVES = 4
+LATE = 1
 MESH = pl.DeviceIdType.MESH
 
 
 def kernel(
-    placement_ref, routes_ref, routes_t_ref, weights_ref, tokens_ref, w_ref, g_ref, m_ref, v_ref,
+    placement_ref, named_ref, gains_ref, tokens_in, w_in, g_in, m_in, v_in,
     mixed_ref, final_ref,
+    tokens_ref, w_ref, g_ref, m_ref, v_ref, total,
     column, served, outgoing, slots, acts, back, spread, landed, chosen,
     ring_send, ring_recv, serve_send, serve_recv, serve_local,
-    tok_send, tok_recv, ret_send, ret_recv, one_send, one_recv, two_send, two_recv, two_local,
+    tok_send, tok_recv, ret_send, ret_recv, one_send, one_recv, two_send, two_recv, two_local, load,
 ):
     dp = lax.axis_index("dp")
     own = lax.axis_index("expert")
@@ -39,6 +41,38 @@
     def slot_rows(p):
         return pl.ds(pl.multiple_of(p * cap, cap), cap)
 
+    loads = [
+        pltpu.make_async_copy(source, target, load.at[i])
+        for i, (source, target) in enumerate(
+            (
+                (w_in, w_ref), (g_in, g_ref), (m_in, m_ref), (v_in, v_ref), (tokens_in, tokens_ref)
+            )
+        )
+    ]
+    for copy in loads:
+        copy.start()
+
+    def place(n):
+        y_step, x_step = n % 4, (n // 4 + n) % 4
+        chip_y, core = (dp // 2 + y_step) % 4, (dp + n // 16) % 2
+        return (chip_y * 2 + core) * X_DIM + (x + x_step) % X_DIM
+
+    def mirror(n):
+        y_step, x_step = (4 - n % 4) % 4, (8 - (n // 4) % 4 - n % 4) % 4
+        return (n // 16) * 16 + ((x_step + 4 - y_step) % 4) * 4 + y_step
+
+    def slot_ids(row):
+        n = row >> 5
+        y_step, x_step = n & 3, ((n >> 2) + n) & 3
+        chip_y, core = (dp // 2 + y_step) & 3, (dp + (n >> 4)) & 1
+        served_by = (chip_y * 2 + core) * X_DIM + ((x + x_step) & 3)
+        return (served_by * cap + (row & (cap - 1))).astype(jnp.float32)
+
+    def owner(n):
+        k = n % Z_DIM
+        z_step = (k % 2) * ((k + 1) // 2) + (1 - k % 2) * (Z_DIM - k // 2)
+        return ((z + z_step) % Z_DIM) * X_DIM + (x + n // Z_DIM + n) % X_DIM
+
     barrier = pltpu.get_barrier_semaphore()
 
     @pl.loop(1, EXPERTS)
@@ -49,6 +83,9 @@
         pl.semaphore_signal(
             barrier, inc=1, device_id=(dp, (own + o) % EXPERTS), device_id_type=MESH
         )
+
+    for copy in loads[:4]:
+        copy.wait()
 
     @pl.loop(0, EXPERTS)
     def _(j):
@@ -142,17 +179,17 @@
 
     tok_count = tokens_ref.shape[0]
 
-    def tok_copy(p, sender):
-        return pltpu.make_async_remote_copy(
-            src_ref=outgoing.at[slot_rows(p), :],
-            dst_ref=slots.at[slot_rows(sender), :],
-            send_sem=tok_send.at[p],
-            recv_sem=tok_recv.at[sender],
-            device_id=plane_peer(p),
-            device_id_type=MESH,
-        )
-
-    named = routes_t_ref[...]
+    def tok_copy(n):
+        return pltpu.make_async_remote_copy(
+            src_ref=outgoing.at[slot_rows(n), :],
+            dst_ref=slots.at[slot_rows(mirror(n)), :],
+            send_sem=tok_send.at[n],
+            recv_sem=tok_recv.at[mirror(n)],
+            device_id=plane_peer(place(n)),
+            device_id_type=MESH,
+        )
+
+    named = named_ref[...]
     ids = lax.broadcasted_iota(jnp.int32, (EXPERTS, tok_count), 0)
     hits = [ids == named[k : k + 1, :] for k in (0, 1)]
     both = jnp.where(hits[0] | hits[1], 1.0, 0.0).astype(jnp.bfloat16)
@@ -165,19 +202,18 @@
         + jnp.sum(jnp.where(hits[k], before, 0.0), axis=0, keepdims=True)
         for k in (0, 1)
     ]
+    loads[4].wait()
     group = 8 * cap
     width = tokens_ref.shape[1]
     chunk = 1024
 
     @pl.loop(0, 4)
     def _(q):
-        first_row = ((dp // 2 + q) % 4) * group
-        slot_id = (first_row + lax.broadcasted_iota(jnp.int32, (group, tok_count), 0)).astype(
-            jnp.float32
-        )
+        row_id = q * group + lax.broadcasted_iota(jnp.int32, (group, tok_count), 0)
+        slot_id = slot_ids(row_id)
         pick = jnp.where((slot_id == wide[0]) | (slot_id == wide[1]), 1.0, 0.0).astype(jnp.bfloat16)
         for c in range(width // chunk):
-            outgoing[pl.ds(pl.multiple_of(first_row, group), group), c * chunk : (c + 1) * chunk] = (
+            outgoing[pl.ds(pl.multiple_of(q * group, group), group), c * chunk : (c + 1) * chunk] = (
                 jnp.dot(
                     pick,
                     tokens_ref[:, c * chunk : (c + 1) * chunk],
@@ -187,15 +223,13 @@
 
         @pl.loop(0, 8)
         def _(i):
-            p = ((dp // 2 + q) % 4) * 8 + (mine + i) % 8
-
-            @pl.when(p != mine)
-            def _():
-                tok_copy(p, mine).start()
-
-            @pl.when(p == mine)
-            def _():
-                slots[slot_rows(mine), :] = outgoing[slot_rows(mine), :]
+            n = q * 8 + i
+
+            @pl.when(n > 0)
+            def _():
+                tok_copy(n).start()
+
+    slots[slot_rows(0), :] = outgoing[slot_rows(0), :]
 
     def one_copy(j, sender):
         return pltpu.make_async_remote_copy(
@@ -219,13 +253,13 @@
 
     two_own = pltpu.make_async_copy(chosen.at[own], final_ref.at[own], two_local)
 
-    ring_waves(0, WAVES // 4)
-
-    @pl.loop(1, EXPERTS)
-    def _(o):
-        one_copy((own + o) % EXPERTS, own).start()
-
-    ring_waves(WAVES // 4, WAVES // 2)
+    ring_waves(0, 1)
+
+    @pl.loop(1, EXPERTS)
+    def _(o):
+        one_copy(owner(o), own).start()
+
+    ring_waves(1, WAVES // 2)
 
     @pl.loop(1, EXPERTS)
     def _(o):
@@ -238,99 +272,123 @@
 
     @pl.loop(1, EXPERTS)
     def _(o):
-        two_copy((own + o) % EXPERTS, own).start()
+        two_copy(owner(o), own).start()
 
     two_own.start()
 
-    @pl.loop(0, DP)
-    def _(s):
-        @pl.when(s != dp)
-        def _():
-            @pl.loop(0, WAVES)
-            def _(h):
-                serve_copy(dp, h, s, s).wait_recv()
-
-        @pl.when(s == dp)
-        def _():
-            @pl.loop(0, WAVES)
-            def _(h):
-                serve_own(h).wait()
-
-    def ret_copy(p, sender):
-        return pltpu.make_async_remote_copy(
-            src_ref=acts.at[slot_rows(p), :],
-            dst_ref=back.at[slot_rows(sender), :],
-            send_sem=ret_send.at[p],
-            recv_sem=ret_recv.at[sender],
-            device_id=plane_peer(p),
-            device_id_type=MESH,
-        )
+    def served_parts(first, last):
+        @pl.loop(0, DP)
+        def _(s):
+            @pl.when(s != dp)
+            def _():
+                @pl.loop(first, last)
+                def _(h):
+                    serve_copy(dp, h, s, s).wait_recv()
+
+            @pl.when(s == dp)
+            def _():
+                @pl.loop(first, last)
+                def _(h):
+                    serve_own(h).wait()
+
+    def product(rows, n, depths):
+        right = jnp.concatenate([served[2 * n, depths, :], served[2 * n + 1, depths, :]], axis=1)
+        return jnp.dot(slots[rows, depths], right, preferred_element_type=jnp.float32)
+
+    early = WAVES - LATE
+    first_depths = slice(0, early * part_rows)
+    last_depths = slice(early * part_rows, width)
+    served_parts(0, early)
 
     @pl.loop(0, 4)
     def _(q):
-        base = ((dp // 2 + q) % 4) * 8
-        rows = pl.ds(pl.multiple_of(base * cap, group), group)
+        base = q * 8
+        rows = pl.ds(pl.multiple_of(q * group, group), group)
 
         @pl.loop(0, 8)
         def _(i):
-            p = base + i
-
-            @pl.when(p != mine)
-            def _():
-                tok_copy(p, p).wait_recv()
+            n = base + i
+
+            @pl.when(n > 0)
+            def _():
+                tok_copy(mirror(n)).wait_recv()
 
         @pl.loop(0, DP // 2)
         def _(n):
-            right = jnp.concatenate([served[2 * n], served[2 * n + 1]], axis=1)
-            total = jnp.dot(slots[rows, :], right, preferred_element_type=jnp.float32)
-            acts[rows, pl.ds(pl.multiple_of(n * 256, 256), 256)] = (
-                total / (1.0 + jnp.exp(-total))
-            ).astype(jnp.bfloat16)
+            total[rows, pl.ds(pl.multiple_of(n * 256, 256), 256)] = product(rows, n, first_depths)
+
+    served_parts(early, WAVES)
+
+    def ret_copy(n):
+        return pltpu.make_async_remote_copy(
+            src_ref=acts.at[slot_rows(n), :],
+            dst_ref=back.at[slot_rows(mirror(n)), :],
+            send_sem=ret_send.at[n],
+            recv_sem=ret_recv.at[mirror(n)],
+            device_id=plane_peer(place(n)),
+            device_id_type=MESH,
+        )
+
+    @pl.loop(0, 4)
+    def _(q):
+        base = q * 8
+        rows = pl.ds(pl.multiple_of(q * group, group), group)
+
+        @pl.loop(0, DP // 2)
+        def _(n):
+            cols = pl.ds(pl.multiple_of(n * 256, 256), 256)
+            value = total[rows, cols] + product(rows, n, last_depths)
+            acts[rows, cols] = (value / (1.0 + jnp.exp(-value))).astype(jnp.bfloat16)
 
         @pl.loop(0, 8)
         def _(i):
-            p = base + (mine + i) % 8
-
-            @pl.when(p != mine)
-            def _():
-                ret_copy(p, mine).start()
-
-            @pl.when(p == mine)
-            def _():
-                back[slot_rows(mine), :] = acts[slot_rows(mine), :]
-
-    tall_named = routes_ref[...]
-    lanes = lax.broadcasted_iota(jnp.int32, (tok_count, EXPERTS), 1)
-    tall_hits = [lanes == tall_named[:, k : k + 1] for k in (0, 1)]
-    tall_both = jnp.where(tall_hits[0] | tall_hits[1], 1.0, 0.0).astype(jnp.bfloat16)
-    later = jnp.where(col < row, 1.0, 0.0).astype(jnp.bfloat16)
-    tall_before = jnp.dot(later, tall_both, preferred_element_type=jnp.float32)
-    slot_lane = lax.broadcasted_iota(jnp.int32, (tok_count, EXPERTS * cap), 1).astype(jnp.float32)
-    tall_pick = []
-    for k in (0, 1):
-        slot = tall_named[:, k : k + 1].astype(jnp.float32) * cap + jnp.sum(
-            jnp.where(tall_hits[k], tall_before, 0.0), axis=1, keepdims=True
-        )
-        tall_pick.append(jnp.where(slot_lane == slot, 1.0, 0.0).astype(jnp.bfloat16))
-
-    @pl.loop(1, EXPERTS)
-    def _(o):
-        p = (mine + EXPERTS - o) % EXPERTS
-        ret_copy(p, p).wait_recv()
-
-    gain = weights_ref[...]
-    for c in range(2):
-        cols = slice(c * 512, (c + 1) * 512)
-        got = [
-            jnp.dot(tall_pick[k], back[:, cols], preferred_element_type=jnp.float32) for k in (0, 1)
-        ]
-        mixed_ref[:, cols] = (gain[:, 0:1] * got[0] + gain[:, 1:2] * got[1]).astype(jnp.bfloat16)
-
-    @pl.loop(1, EXPERTS)
-    def _(o):
-        p = (mine + o) % EXPERTS
-        tok_copy(p, mine).wait_send()
-        ret_copy(p, mine).wait_send()
+            n = base + i
+
+            @pl.when(n > 0)
+            def _():
+                ret_copy(n).start()
+
+    back[slot_rows(0), :] = acts[slot_rows(0), :]
+
+    gains = gains_ref[...]
+    flat = jnp.concatenate(
+        [wide[0], wide[1], gains, jnp.zeros((4, tok_count), jnp.float32)], axis=0
+    )
+    tall = flat.T
+    sums = pl.ds(0, tok_count)
+    total[sums, :] = jnp.zeros((tok_count, total.shape[1]), jnp.float32)
+    lane = lax.broadcasted_iota(jnp.int32, (tok_count, group), 1)
+
+    @pl.loop(0, 4)
+    def _(q):
+        @pl.loop(0, 8)
+        def _(i):
+            n = q * 8 + i
+
+            @pl.when(n > 0)
+            def _():
+                ret_copy(mirror(n)).wait_recv()
+
+        rows = pl.ds(pl.multiple_of(q * group, group), group)
+        slot_id = slot_ids(q * group + lane)
+        for c in range(2):
+            cols = slice(c * 512, (c + 1) * 512)
+            got = [
+                jnp.dot(
+                    jnp.where(slot_id == tall[:, k : k + 1], 1.0, 0.0).astype(jnp.bfloat16),
+                    back[rows, cols],
+                    preferred_element_type=jnp.float32,
+                )
+                for k in (0, 1)
+            ]
+            total[sums, cols] += tall[:, 2:3] * got[0] + tall[:, 3:4] * got[1]
+
+    mixed_ref[...] = total[sums, :].astype(jnp.bfloat16)
+
+    @pl.loop(1, EXPERTS)
+    def _(o):
+        tok_copy(o).wait_send()
+        ret_copy(o).wait_send()
         j = (own + o) % EXPERTS
         one_copy(j, own).wait_send()
         two_copy(j, own).wait_send()
@@ -368,6 +426,7 @@
     cap = 4 * count // EXPERTS
     block = depth // EXPERTS
     vmem = pl.BlockSpec(memory_space=pltpu.VMEM)
+    hbm = pl.BlockSpec(memory_space=pl.ANY)
     dma = pltpu.SemaphoreType.DMA
     mixed, final = pl.pallas_call(
         kernel,
@@ -375,9 +434,14 @@
             jax.ShapeDtypeStruct((count, hidden), jnp.bfloat16),
             jax.ShapeDtypeStruct((EXPERTS, 3 * block, piece), jnp.bfloat16),
         ),
-        in_specs=[pl.BlockSpec(memory_space=pltpu.SMEM)] + [vmem] * 8,
-        out_specs=(vmem, pl.BlockSpec(memory_space=pl.ANY)),
+        in_specs=[pl.BlockSpec(memory_space=pltpu.SMEM)] + [vmem] * 2 + [hbm] * 5,
+        out_specs=(vmem, hbm),
         scratch_shapes=[
+            pltpu.VMEM((count, width), jnp.bfloat16),
+        ]
+        + [pltpu.VMEM((depth, piece), jnp.bfloat16)] * 4
+        + [
+            pltpu.VMEM((EXPERTS * cap, hidden), jnp.float32),
             pltpu.VMEM((Z_DIM, depth, piece), jnp.bfloat16),
             pltpu.VMEM((DP, depth, piece), jnp.bfloat16),
             pltpu.VMEM((EXPERTS * cap, width), jnp.bfloat16),
@@ -394,12 +458,12 @@
             dma((WAVES,)),
         ]
         + [dma((EXPERTS,))] * 8
-        + [dma],
+        + [dma, dma((5,))],
         compiler_params=pltpu.CompilerParams(
             collective_id=0, has_side_effects=True, vmem_limit_bytes=60 * 1024 * 1024
         ),
     )(
-        placement, routes, routes.T, route_weights, tokens,
+        placement, routes.T, route_weights.T, tokens,
         expert_weights[0], grads[0], first_moment[0], second_moment[0],
     )
     state = final.reshape(EXPERTS, 3, block, piece)

time: 262 us -> 250 us (0.954)
  Pallas kernels: 254 us -> 244 us
  local copies, waits for them, and re-layouts: 7.45 us -> 4.5 us
    pallas_call x1, Pallas kernels: 254 us -> 244 us  [shards(): pl.pallas_call(kernel, out_shape=(jax.ShapeDtypeStruct((count, hidden), j...]
    unnamed x5 -> x3, local copies, waits for them, and re-layouts: 3.75 us -> 0.8 us
where the time goes in v4:
time: 250 us; the launch traced here: 249 us
  Pallas kernels  244 us (98%)
  local copies, waits for them, and re-layouts  4.5 us (2%)
    pallas_call x1, Pallas kernels, shards(): pl.pallas_call(kernel, out_shape=(jax.ShapeDtypeStruct((count, hidden), j...  244 us

profile of v4, /device:TPU:1, one launch (start us, length us, event | category | flops | bytes accessed | tf_op | source)
XLA Modules:
  0.0 248.7 jit_solution(10558209008177494864)
XLA Ops:
  0.6 243.6 %shard_map.111 = (bf16[256,1024]{1,0:T(8,128)(2,1)}, bf16[32,384,128]{2,1,0:T(8,128)(2,1)}) custom-call(s32[32]{0:T(128)} %placement_ref.1, s32[2,256]{1,0:T(2,128)} %bitcast.18, f32[2,256]{1,0:T(2,128)} %bitcast.19, bf16[256,4096]{1,0:T(8,128)(2,1)} %tokens_in.1, bf16[4096,128]{1,0:T(8,128)(2,1)} %bitcast.11, bf16[4096,128]{1,0:T(8,128)(2,1)} %bitcast.12, ...), custom_call_target="tpu_custom_call" | custom-call | tf_op jit(solution)/shard_map/pallas_call | solution.py:431
  244.2 0.0 copy-start
  244.2 3.7 %fusion = (bf16[32,1,128,128]{3,2,1,0:T(8,128)(2,1)}, bf16[32,1,128,128]{3,2,1,0:T(8,128)(2,1)}, bf16[32,1,128,128]{3,2,1,0:T(8,128)(2,1)}) fusion(bf16[32,3,128,128]{3,2,1,0:T(8,128)(2,1)} %bitcast.10), kind=kLoop, calls=%fused_computation | loop fusion | bytes 6291456 | tf_op jit(solution)/shard_map/slice | solution.py:470
  247.9 0.0 copy-done
  247.9 0.8 copy.13
Async XLA Ops:
  244.2 3.7 %copy-start = (bf16[256,1024]{1,0:T(8,128)(2,1)S(1)}, bf16[256,1024]{1,0:T(8,128)(2,1)}, u32[]{:S(2)}) copy-start(bf16[256,1024]{1,0:T(8,128)(2,1)} %get-tuple-element.18) | copy-start | bytes 1572868

commit v5 on v4

--- a/solution.py
+++ b/solution.py
@@ -84,25 +84,6 @@
             barrier, inc=1, device_id=(dp, (own + o) % EXPERTS), device_id_type=MESH
         )
 
-    for copy in loads[:4]:
-        copy.wait()
-
-    @pl.loop(0, EXPERTS)
-    def _(j):
-        rows = pl.ds(pl.multiple_of(j * block, block), block)
-        grad = g_ref[rows, :].astype(jnp.float32)
-        first = beta_one * m_ref[rows, :].astype(jnp.float32) + (1.0 - beta_one) * grad
-        second = beta_two * v_ref[rows, :].astype(jnp.float32) + (1.0 - beta_two) * grad * grad
-        updated = w_ref[rows, :].astype(jnp.float32) - learn_rate * first / (
-            jnp.sqrt(second) + adam_eps
-        )
-        updated = updated.astype(jnp.bfloat16)
-        column[z, rows, :] = updated
-        spread[j, 0:block, :] = updated
-        spread[j, block : 2 * block, :] = first.astype(jnp.bfloat16)
-        spread[j, 2 * block : 3 * block, :] = second.astype(jnp.bfloat16)
-
-    landed[own] = spread[own]
     pl.semaphore_wait(barrier, 2 * (EXPERTS - 1))
 
     def part(ref, at, h):
@@ -173,9 +154,6 @@
 
             for parity in (0, 1):
                 ring_hop(3, 2 * v + parity, parity)
-
-    for parity in (0, 1):
-        ring_start(parity)
 
     tok_count = tokens_ref.shape[0]
 
@@ -230,6 +208,28 @@
                 tok_copy(n).start()
 
     slots[slot_rows(0), :] = outgoing[slot_rows(0), :]
+
+    for copy in loads[:4]:
+        copy.wait()
+
+    @pl.loop(0, EXPERTS)
+    def _(j):
+        rows = pl.ds(pl.multiple_of(j * block, block), block)
+        grad = g_ref[rows, :].astype(jnp.float32)
+        first = beta_one * m_ref[rows, :].astype(jnp.float32) + (1.0 - beta_one) * grad
+        second = beta_two * v_ref[rows, :].astype(jnp.float32) + (1.0 - beta_two) * grad * grad
+        updated = w_ref[rows, :].astype(jnp.float32) - learn_rate * first / (
+            jnp.sqrt(second) + adam_eps
+        )
+        updated = updated.astype(jnp.bfloat16)
+        column[z, rows, :] = updated
+        spread[j, 0:block, :] = updated
+        spread[j, block : 2 * block, :] = first.astype(jnp.bfloat16)
+        spread[j, 2 * block : 3 * block, :] = second.astype(jnp.bfloat16)
+
+    landed[own] = spread[own]
+    for parity in (0, 1):
+        ring_start(parity)
 
     def one_copy(j, sender):
         return pltpu.make_async_remote_copy(

time: 250 us -> 256 us (1.024)
  Pallas kernels: 244 us -> 250 us
    pallas_call x1, Pallas kernels: 244 us -> 250 us  [shards(): pl.pallas_call(kernel, out_shape=(jax.ShapeDtypeStruct((count, hidden), j...]
where the time goes in v5:
time: 256 us; the launch traced here: 255 us
  Pallas kernels  250 us (98%)
  local copies, waits for them, and re-layouts  4.5 us (2%)
    pallas_call x1, Pallas kernels, shards(): pl.pallas_call(kernel, out_shape=(jax.ShapeDtypeStruct((count, hidden), j...  250 us

profile of v5, /device:TPU:1, one launch (start us, length us, event | category | flops | bytes accessed | tf_op | source)
XLA Modules:
  0.0 254.9 jit_solution(895599857700188913)
XLA Ops:
  0.6 249.8 %shard_map.111 = (bf16[256,1024]{1,0:T(8,128)(2,1)}, bf16[32,384,128]{2,1,0:T(8,128)(2,1)}) custom-call(s32[32]{0:T(128)} %placement_ref.1, s32[2,256]{1,0:T(2,128)} %bitcast.18, f32[2,256]{1,0:T(2,128)} %bitcast.19, bf16[256,4096]{1,0:T(8,128)(2,1)} %tokens_in.1, bf16[4096,128]{1,0:T(8,128)(2,1)} %bitcast.11, bf16[4096,128]{1,0:T(8,128)(2,1)} %bitcast.12, ...), custom_call_target="tpu_custom_call" | custom-call | tf_op jit(solution)/shard_map/pallas_call | solution.py:431
  250.4 0.0 copy-start
  250.5 3.7 %fusion = (bf16[32,1,128,128]{3,2,1,0:T(8,128)(2,1)}, bf16[32,1,128,128]{3,2,1,0:T(8,128)(2,1)}, bf16[32,1,128,128]{3,2,1,0:T(8,128)(2,1)}) fusion(bf16[32,3,128,128]{3,2,1,0:T(8,128)(2,1)} %bitcast.10), kind=kLoop, calls=%fused_computation | loop fusion | bytes 6291456 | tf_op jit(solution)/shard_map/slice | solution.py:470
  254.2 0.0 copy-done
  254.2 0.8 copy.13
Async XLA Ops:
  250.4 3.7 %copy-start = (bf16[256,1024]{1,0:T(8,128)(2,1)S(1)}, bf16[256,1024]{1,0:T(8,128)(2,1)}, u32[]{:S(2)}) copy-start(bf16[256,1024]{1,0:T(8,128)(2,1)} %get-tuple-element.18) | copy-start | bytes 1572868
